TPU v7x, 128 devices: a whole 4x4x4 slice. The times are simulated.
128 devices in a mesh: row: 8 (over z, core), col: 16 (over x, y).
Axes of the slice: x: 4, y: 4, z: 4, core: 2. Of those that a mesh axis runs over, the one named last changes fastest.
Arguments:
- tokens: bfloat16 [1024, 12288], P('row', 'col'), may hold values from -6 to 6
- up_weight: bfloat16 [1024, 49152], P('row', 'col'), may hold values from -0.1875 to 0.1875
- down_weight: bfloat16 [1024, 49152], P('row', 'col'), may hold values from -0.09375 to 0.09375
- up_index: int32 [8, 384], P(None, 'col'), may hold values from 0 to 95, as said below
- down_index: int32 [8, 384], P(None, 'col'), may hold values from 0 to 95, as said below
- up_bias: float32 [49152], P('col'), may hold values from -3 to 3
- down_bias: float32 [12288], P('col'), may hold values from -3 to 3
Outputs:
- mixed: bfloat16 [1024, 12288], P('row', 'col')
Inputs may be any that keep to these rules, and one draw needn't show every extreme that they name: For each block column c the 8 entries up_index[:, c] are distinct, and for each slot s the entries over any 96 consecutive block columns are distinct. For each block row r the 8 entries down_index[:, r] are distinct, and for each slot s the entries over any 96 consecutive block rows are distinct.
All inputs are finite; a program needn't handle non-finite values.
Results may differ from a plain program's by a relative error of at most 0.015.
Values may be sent and summed in bfloat16 or wider, within the bound.
A program may use at most 128 MiB of HBM per device.

v0:
```python
import jax
import jax.numpy as jnp
from jax import lax
from jax.sharding import PartitionSpec as P

BLK = 128
KB = 8


def per_device(tokens, up_weight, down_weight, up_index, down_index, up_bias, down_bias):
    gathered = lax.all_gather(tokens, "col", axis=1, tiled=True)
    tok_rows = gathered.shape[0]
    dblocks = gathered.shape[1] // BLK
    features = gathered.reshape(tok_rows, dblocks, BLK)
    col_blocks = up_weight.shape[1] // BLK
    block_ids = jnp.arange(dblocks, dtype=jnp.int32)
    zero_pre = jnp.zeros((tok_rows, col_blocks, BLK), jnp.float32)
    running = zero_pre
    panel_rows = lax.all_gather(up_weight, "row", axis=0, tiled=True)
    block_count = panel_rows.shape[0] // BLK
    panels = panel_rows.reshape(block_count, BLK, col_blocks, BLK)
    for add_slot_index in range(block_count):
        selector = (up_index[add_slot_index][:, None] == block_ids[None, :]).astype(jnp.bfloat16)
        selected = jnp.einsum(
            "cd,tdk->tck", selector, features, preferred_element_type=jnp.float32
        ).astype(jnp.bfloat16)
        running = running + jnp.einsum(
            "tck,kcn->tcn", selected, panels[add_slot_index], preferred_element_type=jnp.float32
        )
    preact = running
    preact = preact + up_bias.reshape(col_blocks, BLK)[None]
    hidden = jax.nn.gelu(preact, approximate=True).astype(jnp.bfloat16)
    down_full = lax.all_gather(down_weight, "row", axis=0, tiled=True)
    down_grid = down_full.reshape(KB, BLK, col_blocks, BLK)
    totals = jnp.zeros((dblocks, tok_rows, BLK), jnp.float32)
    for slot_index in range(KB):
        product = jnp.einsum(
            "trk,nrk->rtn", hidden, down_grid[slot_index], preferred_element_type=jnp.float32
        )
        placer = (block_ids[:, None] == down_index[slot_index][None, :]).astype(jnp.float32)
        totals = totals + jnp.einsum(
            "dr,rtn->dtn",
            placer,
            product,
            precision=lax.Precision.HIGHEST,
            preferred_element_type=jnp.float32,
        )
    reduced = lax.psum_scatter(
        totals.astype(jnp.bfloat16), "col", scatter_dimension=0, tiled=True
    ).astype(jnp.float32)
    result = jnp.transpose(reduced, (1, 0, 2)).reshape(tok_rows, -1) + down_bias[None]
    return result.astype(jnp.bfloat16)


def solution(mesh):
    placed = (
        P("row", "col"),
        P("row", "col"),
        P("row", "col"),
        P(None, "col"),
        P(None, "col"),
        P("col"),
        P("col"),
    )
    return jax.shard_map(
        per_device, mesh=mesh, in_specs=placed, out_specs=P("row", "col"), check_vma=False
    )
```

profile of v0, /device:TPU:0, one launch (start us, length us, event | category | flops | bytes accessed | tf_op | source)
XLA Modules:
  0.0 308.1 jit_solution(4415510976900336198)
XLA Ops:
  6.5 0.7 all-gather.4.cloned.1.call-update
  7.3 2.3 copy.47
  9.7 1.2 copy.64
  11.0 49.1 %all-gather.4.cloned.1.call-done = bf16[128,12288]{1,0:T(8,128)(2,1)} async-done(((bf16[128,768]{1,0:T(8,128)(2,1)}), bf16[128,12288]{1,0:T(8,128)(2,1)}) %all-gather.4.cloned.1.call-update) | async-done | bytes 3145744 | tf_op jit(solution)/shard_map/all_gather | solution.py:11
  60.1 2.6 copy.100
  62.7 1.5 fusion.30
  64.2 1.5 fusion.28
  65.7 1.5 fusion.27
  69.6 1.5 fusion.29
  71.1 34.9 %all-gather.6.cloned.1.call-done = bf16[1024,3072]{0,1:T(8,128)(2,1)} async-done(((bf16[128,3072]{0,1:T(8,128)(2,1)}), bf16[1024,3072]{0,1:T(8,128)(2,1)}) %all-gather.6.cloned.1.call-update) | async-done | bytes 6291472 | tf_op jit(solution)/shard_map/all_gather | solution.py:19
  106.0 3.4 %fusion.96 = (bf16[128,3072]{0,1:T(8,128)(2,1)S(1)}, bf16[128,3072]{0,1:T(8,128)(2,1)S(1)}, bf16[128,3072]{0,1:T(8,128)(2,1)S(1)}, bf16[128,3072]{0,1:T(8,128)(2...) fusion(bf16[1024,3072]{0,1:T(8,128)(2,1)} %all-gather.6.cloned., ...), kind=kLoop, calls=%fused_computation.123 | loop fusion | bytes 12582912 | tf_op jit(solution)/shard_map/slice | solution.py:28
  110.6 0.7 fusion.34
  112.3 0.7 fusion.38
  113.0 0.7 fusion.40
  113.7 0.7 fusion.42
  114.3 0.7 fusion.44
  115.5 1.3 fusion.7
  116.7 37.0 %all-gather.8.cloned.1.call-done = bf16[1024,3072]{0,1:T(8,128)(2,1)} async-done(((bf16[128,3072]{0,1:T(8,128)(2,1)}), bf16[1024,3072]{0,1:T(8,128)(2,1)}) %all-gather.8.cloned.1.call-update) | async-done | bytes 6291472 | tf_op jit(solution)/shard_map/all_gather | solution.py:33
  153.7 3.4 %fusion.95 = (bf16[128,3072]{0,1:T(8,128)(2,1)S(1)}, bf16[128,3072]{0,1:T(8,128)(2,1)S(1)}, bf16[128,3072]{0,1:T(8,128)(2,1)S(1)}, bf16[128,3072]{0,1:T(8,128)(2...) fusion(bf16[1024,3072]{0,1:T(8,128)(2,1)} %all-gather.8.cloned., ...), kind=kLoop, calls=%fused_computation.122 | loop fusion | bytes 12582912 | tf_op jit(solution)/shard_map/slice | solution.py:38
  157.5 1.5 fusion.104
  161.3 5.7 %fusion.21 = f32[96,128,128]{2,0,1:T(8,128)} fusion(f32[24,128,128]{2,1,0:T(8,128)S(1)} %fusion.97, s32[24]{0:T(128)S(1)} %get-tuple-element.27), kind=kOutput, calls=%fused_computation.23 | convolution fusion | flops 452987136 | bytes 7864416 | tf_op jit(solution)/shard_map/dr,rtn->dtn/dot_general | solution.py:41
  167.0 5.5 %fusion.19 = f32[96,128,128]{2,0,1:T(8,128)} fusion(f32[24,128,128]{2,1,0:T(8,128)S(1)} %fusion.98, s32[24]{0:T(128)S(1)} %get-tuple-element.26), kind=kOutput, calls=%fused_computation.21 | convolution fusion | flops 452987136 | bytes 7864416 | tf_op jit(solution)/shard_map/dr,rtn->dtn/dot_general | solution.py:41
  172.5 5.5 %fusion.17 = f32[96,128,128]{2,0,1:T(8,128)} fusion(f32[24,128,128]{2,1,0:T(8,128)S(1)} %fusion.99, s32[24]{0:T(128)S(1)} %get-tuple-element.25), kind=kOutput, calls=%fused_computation.19 | convolution fusion | flops 452987136 | bytes 7864416 | tf_op jit(solution)/shard_map/dr,rtn->dtn/dot_general | solution.py:41
  178.0 5.5 %fusion.15 = f32[96,128,128]{2,0,1:T(8,128)} fusion(f32[24,128,128]{2,1,0:T(8,128)S(1)} %fusion.100, s32[24]{0:T(128)S(1)} %get-tuple-element.24), kind=kOutput, calls=%fused_computation.17 | convolution fusion | flops 452987136 | bytes 7864416 | tf_op jit(solution)/shard_map/dr,rtn->dtn/dot_general | solution.py:41
  183.5 5.4 %fusion.13 = f32[96,128,128]{2,0,1:T(8,128)} fusion(f32[24,128,128]{2,1,0:T(8,128)S(1)} %fusion.101, s32[24]{0:T(128)S(1)} %get-tuple-element.23), kind=kOutput, calls=%fused_computation.15 | convolution fusion | flops 452987136 | bytes 7864416 | tf_op jit(solution)/shard_map/dr,rtn->dtn/dot_general | solution.py:41
  189.0 5.5 %fusion.11 = f32[96,128,128]{2,0,1:T(8,128)} fusion(f32[24,128,128]{2,1,0:T(8,128)S(1)} %fusion.102, s32[24]{0:T(128)S(1)} %get-tuple-element.22), kind=kOutput, calls=%fused_computation.13 | convolution fusion | flops 452987136 | bytes 7864416 | tf_op jit(solution)/shard_map/dr,rtn->dtn/dot_general | solution.py:41
  194.4 5.5 %fusion.9 = f32[96,128,128]{2,0,1:T(8,128)} fusion(f32[24,128,128]{2,1,0:T(8,128)S(1)} %fusion.103, s32[24]{0:T(128)S(1)} %get-tuple-element.28), kind=kOutput, calls=%fused_computation.11 | convolution fusion | flops 452987136 | bytes 7864416 | tf_op jit(solution)/shard_map/dr,rtn->dtn/dot_general | solution.py:41
  199.9 20.0 %add_convert_fusion = bf16[96,128,128]{2,0,1:T(8,128)(2,1)S(1)} fusion(f32[96,128,128]{2,0,1:T(8,128)} %fusion.9, f32[96,128,128]{2,0,1:T(8,128)} %fusion.11, f32[96,128,128]{2,0,1:T(8,128)} %fusion.13, f32[96,128,128]{2,0,1:T(8,128)} %fusion.15, f32[96,128,128]{2,0,1:T(8,128)} %fusion.17, f32[96,128,128]{2,0,1:T(8,128)} %fusion.21, ...), kind=kOutput, calls=%fused_computation | convolution fusion | flops 465570048 | bytes 48758880 | tf_op jit(solution)/shard_map/dr,rtn->dtn/dot_general | solution.py:41
  219.9 2.9 copy.81
  222.8 76.7 %reduce-scatter.2.cloned.1.call-done = bf16[6,128,128]{2,1,0:T(8,128)(2,1)} async-done(((bf16[96,128,128]{2,1,0:T(8,128)(2,1)}), bf16[6,128,128]{2,1,0:T(8,128)(2,1)}) %reduce-scatter.2.cloned.1.call-update) | async-done | bytes 196624 | tf_op jit(solution)/shard_map/reduce_scatter | solution.py:48
  299.5 1.1 copy.82
  300.8 0.8 copy.83
  (41 shorter events, 8.1 us)
Async XLA Ops:
  6.5 3.2 %copy-start.4 = (bf16[128,3072]{1,0:T(8,128)(2,1)S(1)}, bf16[128,3072]{1,0:T(8,128)(2,1)}, u32[]{:S(2)}) copy-start(bf16[128,3072]{1,0:T(8,128)(2,1)} %param.9) | copy-start | bytes 2359300
  6.5 53.6 %all-gather.4.cloned.1.call-start = ((), (), s32[]{:S(2)}) async-start(), calls=%async_computation.1 | async-start | bytes 3342336 | tf_op jit(solution)/shard_map/all_gather | solution.py:11
  7.3 98.7 %all-gather.6.cloned.1.call-start = ((), (), s32[]{:S(2)}) async-start(), calls=%async_computation.2 | async-start | bytes 7077888 | tf_op jit(solution)/shard_map/all_gather | solution.py:19
  9.6 1.3 copy-start.7
  9.6 1.4 copy-start.8
  9.6 144.1 %all-gather.8.cloned.1.call-start = ((), (), s32[]{:S(2)}) async-start(), calls=%async_computation.3 | async-start | bytes 7077888 | tf_op jit(solution)/shard_map/all_gather | solution.py:33
  10.9 288.6 %reduce-scatter.2.cloned.1.call-start = ((), (), s32[]{:S(2)}) async-start(), calls=%async_computation.4 | async-start | bytes 3342336 | tf_op jit(solution)/shard_map/reduce_scatter | solution.py:48
  106.0 3.4 %copy-start.2 = (bf16[128,24,128]{2,1,0:T(8,128)(2,1)S(1)}, bf16[128,24,128]{2,1,0:T(8,128)(2,1)}, u32[]{:S(2)}) copy-start(bf16[128,24,128]{2,1,0:T(8,128)(2,1)} %fusion.29) | copy-start | bytes 2359300
  109.4 1.1 copy-start.1
  110.6 1.1 copy-start
  114.3 1.1 copy-start.3
  114.3 1.1 copy-start.5
  222.8 77.8 %copy-start.6 = (f32[768]{0:T(1024)S(1)}, f32[768]{0:T(1024)}, u32[]{:S(2)}) copy-start(f32[768]{0:T(1024)} %param.13) | copy-start | bytes 9220
Sparse Core Ops, SparseCore 0:
  9.6 50.4 all-gather.3
  61.8 44.1 all-gather.5
  107.7 46.0 all-gather.7
  222.9 76.5 reduce-scatter.1
where the time goes:
time: 308 us
  waiting for transfers between devices  198 us (64%)
  matrix products  77 us (25%)
  local copies, waits for them, and re-layouts  19.1 us (6%)
  between operations  13.3 us (4%)
    reduce_scatter x1, waiting for transfers between devices, per_device(): lax.psum_scatter(totals.astype(jnp.bfloat16), 'col', scatter_dimension=0,...  76.7 us
    dot_general x8, matrix products, per_device(): jnp.einsum('dr,rtn->dtn', placer, product, precision=lax.Precision.HIGHES...  58.6 us
    all_gather x1, waiting for transfers between devices, per_device(): gathered = lax.all_gather(tokens, 'col', axis=1, tiled=True)  49.1 us
    all_gather x1, waiting for transfers between devices, per_device(): down_full = lax.all_gather(down_weight, 'row', axis=0, tiled=True)  37 us
    all_gather x1, waiting for transfers between devices, per_device(): panel_rows = lax.all_gather(up_weight, 'row', axis=0, tiled=True)  34.9 us
    dot_general x8, matrix products, per_device(): jnp.einsum('cd,tdk->tck', selector, features, preferred_element_type=jnp....  8.36 us
    unnamed x21, local copies, waits for them, and re-layouts  7.5 us
  transfers between devices with their start and end apart: 4, of which 4 were waited for; matrix products, arithmetic and copies ran while one was open for 8% of the time, Pallas kernels for 0%

commit v1 on v0

--- a/solution.py
+++ b/solution.py
@@ -8,7 +8,16 @@
 
 
 def per_device(tokens, up_weight, down_weight, up_index, down_index, up_bias, down_bias):
-    gathered = lax.all_gather(tokens, "col", axis=1, tiled=True)
+
+    def save_the_masks(inputs):
+        how_many = lax.axis_size("col")
+        near = range(inputs.ndim)
+        e_next = map(lambda w: how_many if w == 1 else 1, near)
+        views = list(e_next)
+        w_next = jnp.tile(inputs, views)
+        return lax.all_to_all(w_next, axis_name="col", split_axis=1, concat_axis=1, tiled=True)
+
+    gathered = save_the_masks(tokens)
     tok_rows = gathered.shape[0]
     dblocks = gathered.shape[1] // BLK
     features = gathered.reshape(tok_rows, dblocks, BLK)

time: 308 us -> 259 us (0.84)
  waiting for transfers between devices: 198 us -> 128 us
  local copies, waits for them, and re-layouts: 19.1 us -> 29.3 us
  starting transfers between devices: 0.13 us -> 7.33 us
  matrix products: 77 us -> 80.6 us
    all_gather x1 -> x0, waiting for transfers between devices: 49.1 us -> none  [per_device(): gathered = lax.all_gather(tokens, 'col', axis=1, tiled=True)]
    all_to_all x0 -> x1, waiting for transfers between devices: none -> 42.4 us  [save_the_masks(): lax.all_to_all(w_next, axis_name='col', split_axis=1, concat_axis=1, tile...]
    all_gather x1, waiting for transfers between devices: 34.9 us -> 0.01 us  [per_device(): panel_rows = lax.all_gather(up_weight, 'row', axis=0, tiled=True)]
    all_gather x1, waiting for transfers between devices: 37 us -> 9.05 us  [per_device(): down_full = lax.all_gather(down_weight, 'row', axis=0, tiled=True)]
    all_to_all x0 -> x1, starting transfers between devices: none -> 7.25 us  [save_the_masks(): lax.all_to_all(w_next, axis_name='col', split_axis=1, concat_axis=1, tile...]
    reshape x0 -> x1, local copies, waits for them, and re-layouts: none -> 5.17 us  [per_device(): features = gathered.reshape(tok_rows, dblocks, BLK)]
    dot_general x8, matrix products: 8.36 us -> 11.9 us  [per_device(): jnp.einsum('cd,tdk->tck', selector, features, preferred_element_type=jnp....]
    all_to_all x0 -> x1, local copies, waits for them, and re-layouts: none -> 3.39 us  [save_the_masks(): lax.all_to_all(w_next, axis_name='col', split_axis=1, concat_axis=1, tile...]
  transfers between devices with their start and end apart: 4 -> 4, of which waited for: 4 -> 3; matrix products, arithmetic and copies ran while one was open for 8% -> 13% of each run, Pallas kernels for 0% -> 0%
where the time goes in v1:
time: 259 us
  waiting for transfers between devices  128 us (49%)
  matrix products  80.6 us (31%)
  local copies, waits for them, and re-layouts  29.3 us (11%)
  between operations  13.3 us (5%)
  starting transfers between devices  7.33 us (3%)
    reduce_scatter x1, waiting for transfers between devices, per_device(): lax.psum_scatter(totals.astype(jnp.bfloat16), 'col', scatter_dimension=0,...  76.7 us
    dot_general x8, matrix products, per_device(): jnp.einsum('dr,rtn->dtn', placer, product, precision=lax.Precision.HIGHES...  58.6 us
    all_to_all x1, waiting for transfers between devices, save_the_masks(): lax.all_to_all(w_next, axis_name='col', split_axis=1, concat_axis=1, tile...  42.4 us
    dot_general x8, matrix products, per_device(): jnp.einsum('cd,tdk->tck', selector, features, preferred_element_type=jnp....  11.9 us
    all_gather x1, waiting for transfers between devices, per_device(): down_full = lax.all_gather(down_weight, 'row', axis=0, tiled=True)  9.05 us
    all_to_all x1, starting transfers between devices, save_the_masks(): lax.all_to_all(w_next, axis_name='col', split_axis=1, concat_axis=1, tile...  7.25 us
    unnamed x30, local copies, waits for them, and re-layouts  6.92 us
    dot_general x8, matrix products, per_device(): jnp.einsum('tck,kcn->tcn', selected, panels[add_slot_index], preferred_el...  5.84 us
  transfers between devices with their start and end apart: 4, of which 3 were waited for; matrix products, arithmetic and copies ran while one was open for 13% of the time, Pallas kernels for 0%

profile of v1, /device:TPU:0, one launch (start us, length us, event | category | flops | bytes accessed | tf_op | source)
XLA Modules:
  0.0 258.8 jit_solution(4070106358747659434)
XLA Ops:
  6.5 2.4 copy.49
  9.0 1.2 copy.66
  10.2 2.0 tile.2
  12.1 7.2 %all-to-all-start = ((bf16[128,16,768]{2,0,1:T(8,128)(2,1)}), bf16[128,16,768]{2,0,1:T(8,128)(2,1)S(1)}, u32[]{:S(2)}, u32[]{:S(2)}) async-start(bf16[128,16,768]{2,0,1:T(8,128)(2,1)} %tile.2), calls=%async_computation | async-start | bytes 6291456 | tf_op jit(solution)/shard_map/all_to_all | solution.py:18
  19.5 42.4 %all-to-all-done = bf16[128,16,768]{2,0,1:T(8,128)(2,1)S(1)} async-done(((bf16[128,16,768]{2,0,1:T(8,128)(2,1)}), bf16[128,16,768]{2,0,1:T(8,128)(2,1)S(1)}, u32[]{:S(2)}, u32[]{:S(2)}) %all-to-all-start) | async-done | bytes 3145760 | tf_op jit(solution)/shard_map/all_to_all | solution.py:18
  61.9 3.4 %copy.48 = bf16[128,16,768]{2,1,0:T(8,128)(2,1)} copy(bf16[128,16,768]{2,0,1:T(8,128)(2,1)S(1)} %all-to-all-done) | data formatting | bytes 6291456 | tf_op jit(solution)/shard_map/all_to_all | solution.py:18
  65.3 5.2 %reshape.61 = bf16[128,96,128]{2,1,0:T(8,128)(2,1)S(1)} reshape(bf16[128,16,768]{2,1,0:T(8,128)(2,1)} %copy.48) | data formatting | bytes 6291456 | tf_op jit(solution)/shard_map/reshape | solution.py:23
  70.4 1.5 fusion.30
  72.0 1.5 fusion.29
  73.5 1.5 fusion.28
  75.0 1.5 fusion.27
  76.5 1.5 fusion.26
  77.9 1.5 fusion.25
  79.4 1.5 fusion.24
  80.9 1.5 fusion.23
  82.4 3.7 %fusion.96 = (bf16[128,3072]{0,1:T(8,128)(2,1)S(1)}, bf16[128,3072]{0,1:T(8,128)(2,1)S(1)}, bf16[128,3072]{0,1:T(8,128)(2,1)S(1)}, bf16[128,3072]{0,1:T(8,128)(2...) fusion(bf16[1024,3072]{0,1:T(8,128)(2,1)} %all-gather.3.cloned., ...), kind=kLoop, calls=%fused_computation.123 | loop fusion | bytes 12582912 | tf_op jit(solution)/shard_map/slice | solution.py:37
  94.1 1.3 fusion.7
  95.4 9.1 %all-gather.5.cloned.1.call-done = bf16[1024,3072]{0,1:T(8,128)(2,1)} async-done(((bf16[128,3072]{0,1:T(8,128)(2,1)}), bf16[1024,3072]{0,1:T(8,128)(2,1)}) %all-gather.5.cloned.1.call-update) | async-done | bytes 6291472 | tf_op jit(solution)/shard_map/all_gather | solution.py:42
  104.4 3.4 %fusion.95 = (bf16[128,3072]{0,1:T(8,128)(2,1)S(1)}, bf16[128,3072]{0,1:T(8,128)(2,1)S(1)}, bf16[128,3072]{0,1:T(8,128)(2,1)S(1)}, bf16[128,3072]{0,1:T(8,128)(2...) fusion(bf16[1024,3072]{0,1:T(8,128)(2,1)} %all-gather.5.cloned., ...), kind=kLoop, calls=%fused_computation.122 | loop fusion | bytes 12582912 | tf_op jit(solution)/shard_map/slice | solution.py:47
  107.8 1.5 fusion.104
  112.0 5.7 %fusion.21 = f32[96,128,128]{2,0,1:T(8,128)} fusion(f32[24,128,128]{2,1,0:T(8,128)S(1)} %fusion.97, s32[24]{0:T(128)S(1)} %get-tuple-element.27), kind=kOutput, calls=%fused_computation.23 | convolution fusion | flops 452987136 | bytes 7864416 | tf_op jit(solution)/shard_map/dr,rtn->dtn/dot_general | solution.py:50
  117.8 5.5 %fusion.19 = f32[96,128,128]{2,0,1:T(8,128)} fusion(f32[24,128,128]{2,1,0:T(8,128)S(1)} %fusion.98, s32[24]{0:T(128)S(1)} %get-tuple-element.26), kind=kOutput, calls=%fused_computation.21 | convolution fusion | flops 452987136 | bytes 7864416 | tf_op jit(solution)/shard_map/dr,rtn->dtn/dot_general | solution.py:50
  123.2 5.5 %fusion.17 = f32[96,128,128]{2,0,1:T(8,128)} fusion(f32[24,128,128]{2,1,0:T(8,128)S(1)} %fusion.99, s32[24]{0:T(128)S(1)} %get-tuple-element.25), kind=kOutput, calls=%fused_computation.19 | convolution fusion | flops 452987136 | bytes 7864416 | tf_op jit(solution)/shard_map/dr,rtn->dtn/dot_general | solution.py:50
  128.7 5.5 %fusion.15 = f32[96,128,128]{2,0,1:T(8,128)} fusion(f32[24,128,128]{2,1,0:T(8,128)S(1)} %fusion.100, s32[24]{0:T(128)S(1)} %get-tuple-element.24), kind=kOutput, calls=%fused_computation.17 | convolution fusion | flops 452987136 | bytes 7864416 | tf_op jit(solution)/shard_map/dr,rtn->dtn/dot_general | solution.py:50
  134.2 5.4 %fusion.13 = f32[96,128,128]{2,0,1:T(8,128)} fusion(f32[24,128,128]{2,1,0:T(8,128)S(1)} %fusion.101, s32[24]{0:T(128)S(1)} %get-tuple-element.23), kind=kOutput, calls=%fused_computation.15 | convolution fusion | flops 452987136 | bytes 7864416 | tf_op jit(solution)/shard_map/dr,rtn->dtn/dot_general | solution.py:50
  139.7 5.5 %fusion.11 = f32[96,128,128]{2,0,1:T(8,128)} fusion(f32[24,128,128]{2,1,0:T(8,128)S(1)} %fusion.102, s32[24]{0:T(128)S(1)} %get-tuple-element.22), kind=kOutput, calls=%fused_computation.13 | convolution fusion | flops 452987136 | bytes 7864416 | tf_op jit(solution)/shard_map/dr,rtn->dtn/dot_general | solution.py:50
  145.1 5.5 %fusion.9 = f32[96,128,128]{2,0,1:T(8,128)} fusion(f32[24,128,128]{2,1,0:T(8,128)S(1)} %fusion.103, s32[24]{0:T(128)S(1)} %get-tuple-element.28), kind=kOutput, calls=%fused_computation.11 | convolution fusion | flops 452987136 | bytes 7864416 | tf_op jit(solution)/shard_map/dr,rtn->dtn/dot_general | solution.py:50
  150.6 20.0 %add_convert_fusion = bf16[96,128,128]{2,0,1:T(8,128)(2,1)S(1)} fusion(f32[96,128,128]{2,0,1:T(8,128)} %fusion.9, f32[96,128,128]{2,0,1:T(8,128)} %fusion.11, f32[96,128,128]{2,0,1:T(8,128)} %fusion.13, f32[96,128,128]{2,0,1:T(8,128)} %fusion.15, f32[96,128,128]{2,0,1:T(8,128)} %fusion.17, f32[96,128,128]{2,0,1:T(8,128)} %fusion.21, ...), kind=kOutput, calls=%fused_computation | convolution fusion | flops 465570048 | bytes 48758880 | tf_op jit(solution)/shard_map/dr,rtn->dtn/dot_general | solution.py:50
  170.6 2.8 %copy.83 = bf16[96,128,128]{2,1,0:T(8,128)(2,1)} copy(bf16[96,128,128]{2,0,1:T(8,128)(2,1)S(1)} %add_convert_fusion) | data formatting | bytes 6291456 | tf_op jit(solution)/shard_map/convert_element_type | solution.py:58
  173.5 76.7 %reduce-scatter.2.cloned.1.call-done = bf16[6,128,128]{2,1,0:T(8,128)(2,1)} async-done(((bf16[96,128,128]{2,1,0:T(8,128)(2,1)}), bf16[6,128,128]{2,1,0:T(8,128)(2,1)}) %reduce-scatter.2.cloned.1.call-update) | async-done | bytes 196624 | tf_op jit(solution)/shard_map/reduce_scatter | solution.py:57
  250.2 1.1 copy.84
  251.4 0.8 copy.85
  (52 shorter events, 11.0 us)
Async XLA Ops:
  6.5 2.4 copy-start.8
  6.5 75.8 %all-gather.3.cloned.1.call-start = ((), (), s32[]{:S(2)}) async-start(), calls=%async_computation.2 | async-start | bytes 7077888 | tf_op jit(solution)/shard_map/all_gather | solution.py:28
  8.9 1.3 copy-start.9
  8.9 95.5 %all-gather.5.cloned.1.call-start = ((), (), s32[]{:S(2)}) async-start(), calls=%async_computation.3 | async-start | bytes 7077888 | tf_op jit(solution)/shard_map/all_gather | solution.py:42
  12.1 7.3 %copy-start.12 = (s32[8,24]{1,0:T(8,128)S(1)}, s32[8,24]{1,0:T(8,128)}, u32[]{:S(2)}) copy-start(s32[8,24]{1,0:T(8,128)} %param.10) | copy-start | bytes 2308
  12.1 7.3 %copy-start.13 = (s32[8,24]{1,0:T(8,128)S(1)}, s32[8,24]{1,0:T(8,128)}, u32[]{:S(2)}) copy-start(s32[8,24]{1,0:T(8,128)} %param.11) | copy-start | bytes 2308
  12.1 49.7 %all-to-all-start = ((bf16[128,16,768]{2,0,1:T(8,128)(2,1)}), bf16[128,16,768]{2,0,1:T(8,128)(2,1)S(1)}, u32[]{:S(2)}, u32[]{:S(2)}) async-start(bf16[128,16,768]{2,0,1:T(8,128)(2,1)} %tile.2), calls=%async_computation | async-start | bytes 6291456 | tf_op jit(solution)/shard_map/all_to_all | solution.py:18
  19.4 230.8 %reduce-scatter.2.cloned.1.call-start = ((), (), s32[]{:S(2)}) async-start(), calls=%async_computation.4 | async-start | bytes 3342336 | tf_op jit(solution)/shard_map/reduce_scatter | solution.py:57
  82.4 3.7 %copy-start.6 = (bf16[128,24,128]{2,1,0:T(8,128)(2,1)S(1)}, bf16[128,24,128]{2,1,0:T(8,128)(2,1)}, u32[]{:S(2)}) copy-start(bf16[128,24,128]{2,1,0:T(8,128)(2,1)} %fusion.29) | copy-start | bytes 2359300
  86.1 1.1 copy-start.5
  87.3 1.1 copy-start.3
  88.4 1.1 copy-start.2
  89.5 1.1 copy-start.1
  90.7 1.1 copy-start.4
  91.8 1.1 copy-start
  92.9 1.2 copy-start.7
  92.9 1.2 copy-start.10
  173.5 77.8 %copy-start.11 = (f32[768]{0:T(1024)S(1)}, f32[768]{0:T(1024)}, u32[]{:S(2)}) copy-start(f32[768]{0:T(1024)} %param.13) | copy-start | bytes 9220
Sparse Core Ops, SparseCore 0:
  9.0 47.6 all-gather.2
  58.4 45.9 all-gather.4
  173.6 76.4 reduce-scatter.1
